TPU v7x, 128 devices: a whole 4x4x4 slice. The times are simulated.
128 devices in a mesh: dp: 16 (over y_hi, z, core), shard: 8 (over x, y_lo).
Axes of the slice: x: 4, y: 4 (y_hi: 2, y_lo: 2; y = y_hi * 2 + y_lo), z: 4, core: 2. Of those that a mesh axis runs over, the one named last changes fastest.
Arguments:
- queries: float32 [65536, 256], P(('dp', 'shard'))
- items: float32 [163840, 256], P('shard')
- positive: int32 [65536], P(('dp', 'shard')), may hold values from 0 to 163839
- tile_ids: int32 [128, 8, 3], P(('dp', 'shard')), may hold values from 0 to 39, as said below
- counts: int32 [128, 8], P(('dp', 'shard')), may hold values from 1 to 3, as said below
Outputs:
- loss: float32 [65536], P(('dp', 'shard'))
- query_grad: float32 [65536, 256], P(('dp', 'shard'))
- item_grad: float32 [163840, 256], P(('shard', 'dp'))
Inputs may be any that keep to these rules, and one draw needn't show every extreme that they name: `tile_ids`: within one block and shard the 3 entries are distinct; only the first counts of them are visited. `counts`: every block visits exactly 3 tiles on at least one shard.
All inputs are finite; a program needn't handle non-finite values.
Results may differ from a plain program's by a relative error of at most 0.0003.
Values sent between devices are 32-bit elements; how exact they have to be, the bound alone decides.
A program may use at most 192 MiB of HBM per device.

v0:
```python
import jax
import jax.numpy as jnp
from jax import lax
from jax.sharding import PartitionSpec as P

TILE = 512


very_low = -1e30


def joined(part, axis, combine):
    gathered = jax.tree.map(lambda a: lax.all_gather(a, axis), part)

    def take(source):
        return jax.tree.map(lambda a: lax.dynamic_index_in_dim(a, source, 0, False), gathered)

    return lax.fori_loop(
        1, lax.axis_size(axis), lambda source, state: combine(state, take(source)), take(0)
    )


def positive_row(qblk, pblk, items, shard_at):
    local_rows = items.shape[0]
    offset = pblk - shard_at * local_rows
    inside = (offset >= 0) & (offset < local_rows)
    safe = jnp.clip(offset, 0, local_rows - 1)
    target = jnp.where(inside, offset, local_rows)
    chosen = jnp.take(items, safe, axis=0)
    logit = jnp.where(inside, jnp.sum(qblk * chosen, axis=1), 0.0)
    return (inside, target, chosen, logit)


def tile_logits(qblk, items, tile):
    block = lax.dynamic_slice_in_dim(items, tile * TILE, TILE, 0)
    logits = jnp.einsum(
        "qd,td->qt",
        qblk,
        block,
        precision=lax.Precision.HIGHEST,
        preferred_element_type=jnp.float32,
    )
    return (logits, block)


def block_stats(qblk, pblk, idrow, count, items, shard_at):
    rows = qblk.shape[0]

    def visit(step, carry):
        top, total = carry
        logits, block = tile_logits(qblk, items, idrow[step])
        new_top = jnp.maximum(top, jnp.max(logits, axis=1))
        total = total * jnp.exp(top - new_top) + jnp.sum(jnp.exp(logits - new_top[:, None]), axis=1)
        return (new_top, total)

    start = (jnp.full((rows,), very_low, jnp.float32), jnp.zeros((rows,), jnp.float32))
    top, total = lax.fori_loop(0, count, visit, start)
    inside, target, chosen, logit = positive_row(qblk, pblk, items, shard_at)
    new_top = jnp.maximum(top, jnp.where(inside, logit, very_low))
    total = total * jnp.exp(top - new_top) + jnp.where(inside, jnp.exp(logit - new_top), 0.0)
    return ((new_top, total, logit), (inside, target, chosen))


def block_grads(qblk, idrow, count, lse, items, d_local, inside, chosen, plogit):
    high = lax.Precision.HIGHEST

    def visit(step, carry):
        dq, grads = carry
        tile = idrow[step]
        logits, block = tile_logits(qblk, items, tile)
        prob = jnp.exp(logits - lse[:, None])
        dq = dq + jnp.dot(prob, block, precision=high, preferred_element_type=jnp.float32)
        update = jnp.einsum(
            "qt,qd->td", prob, qblk, precision=high, preferred_element_type=jnp.float32
        )
        current = lax.dynamic_slice_in_dim(grads, tile * TILE, TILE, 0)
        grads = lax.dynamic_update_slice_in_dim(grads, current + update, tile * TILE, 0)
        return (dq, grads)

    dq, d_local = lax.fori_loop(0, count, visit, (jnp.zeros(qblk.shape, jnp.float32), d_local))
    weight = jnp.where(inside, jnp.exp(plogit - lse) - 1.0, 0.0)
    dq = dq + weight[:, None] * chosen
    return (dq, d_local, weight[:, None] * qblk)


def combine_stats(first, second):
    top = jnp.maximum(first[0], second[0])
    total = first[1] * jnp.exp(first[0] - top) + second[1] * jnp.exp(second[0] - top)
    return (top, total, first[2] + second[2])


def local(queries, items, positive, tile_ids, counts):
    shard_at = lax.axis_index("shard")
    n_shard = lax.axis_size("shard")
    rows = queries.shape[0]
    width = queries.shape[1]
    seen_q, seen_pos, seen_ids, seen_cnt = (
        lax.all_gather(queries, "shard", axis=0, tiled=True),
        lax.all_gather(positive, "shard", axis=0, tiled=True),
        lax.all_gather(tile_ids, "shard", axis=0, tiled=True),
        lax.all_gather(counts, "shard", axis=0, tiled=True),
    )
    seen_q = seen_q.reshape(n_shard, rows, width)
    seen_pos = seen_pos.reshape(n_shard, rows)
    idrows = jnp.take(seen_ids, shard_at, axis=1)
    seen_counts = jnp.take(seen_cnt, shard_at, axis=1)

    def stats_of(xs):
        return block_stats(xs[0], xs[1], xs[2], xs[3], items, shard_at)

    (tops, totals, plogs), (insides, targets, chosens) = lax.map(
        stats_of, (seen_q, seen_pos, idrows, seen_counts)
    )
    local_plogs = plogs
    tops, totals, plogs = joined((tops, totals, plogs), "shard", combine_stats)
    lse = tops + jnp.log(totals)
    loss = jnp.take(lse, shard_at, axis=0) - jnp.take(plogs, shard_at, axis=0)
    d_local = jnp.zeros(items.shape, jnp.float32)

    def grads_of(grads, xs):
        dq, grads, update = block_grads(
            xs[0], xs[1], xs[2], xs[3], items, grads, xs[4], xs[5], xs[6]
        )
        return (grads, (dq, update))

    d_local, (dq_parts, updates) = lax.scan(
        grads_of, d_local, (seen_q, idrows, seen_counts, lse, insides, chosens, local_plogs)
    )
    d_local = d_local.at[targets.reshape(-1)].add(updates.reshape(-1, width), mode="drop")
    query_grad = lax.psum_scatter(dq_parts, "shard", scatter_dimension=0, tiled=True).reshape(
        rows, width
    )
    item_grad = lax.psum_scatter(d_local, "dp", scatter_dimension=0, tiled=True)
    return (loss, query_grad, item_grad)


def solution(mesh):
    placed = (
        P(("dp", "shard"), None),
        P("shard", None),
        P(("dp", "shard")),
        P(("dp", "shard"), None, None),
        P(("dp", "shard"), None),
    )
    return jax.shard_map(
        local,
        mesh=mesh,
        in_specs=placed,
        out_specs=(P(("dp", "shard")), P(("dp", "shard"), None), P(("shard", "dp"), None)),
        check_vma=False,
    )
```

profile of v0, /device:TPU:1, one launch (start us, length us, event | category | flops | bytes accessed | tf_op | source)
XLA Modules:
  0.0 876.5 jit_solution(1433341906452066203)
XLA Ops:
  8.7 22.8 %all_gather.31 = s32[8,8,3]{1,2,0:T(4,128)S(1)} all-gather(s32[1,8,3]{1,2,0:T(4,128)S(1)} %copy.12), channel_id=1, replica_groups=mesh['dp'=16,'shard'=8] {'shard'}, dimensions={0}, use_global_device_ids=true | all-gather | bytes 864 | tf_op jit(solution)/shard_map/all_gather | solution.py:100
  31.8 25.3 %all-gather.4 = s32[8,1,512]{2,1,0:T(1,128)S(1)} all-gather(s32[1,1,512]{2,1,0:T(1,128)} %bitcast.138), channel_id=1, replica_groups=mesh['dp'=16,'shard'=8] {'shard'}, dimensions={0}, use_global_device_ids=true | all-gather | bytes 18432 | tf_op jit(solution)/shard_map/all_gather | solution.py:99
  57.1 14.5 %all-gather.3 = s32[8,1,8]{2,1,0:T(1,128)S(1)} all-gather(s32[1,1,8]{2,1,0:T(1,128)} %bitcast.139), channel_id=1, replica_groups=mesh['dp'=16,'shard'=8] {'shard'}, dimensions={0}, use_global_device_ids=true | all-gather | bytes 288 | tf_op jit(solution)/shard_map/all_gather | solution.py:101
  71.8 31.3 %all-gather.7.cloned.1.call-done = f32[4096,256]{1,0:T(8,128)} async-done(((f32[512,256]{1,0:T(8,128)}), f32[4096,256]{1,0:T(8,128)}) %all-gather.7.cloned.1.call-update) | async-done | bytes 4194320 | tf_op jit(solution)/shard_map/all_gather | solution.py:98
  105.5 157.3 %while.103 = (s32[]{:T(128)}, f32[8,512]{1,0:T(8,128)S(1)}, f32[8,512]{1,0:T(8,128)S(1)}, f32[8,512]{1,0:T(8,128)S(1)}, pred[8,512]{1,0:T(8,128)(4,1)S(1)}, /*in...) while((s32[]{:T(128)}, f32[8,512]{1,0:T(8,128)S(1)}, ...), condition=%wide.region_6.7_spmd, body=%wide.region_0.6_spmd.sunk | while | flops 806631936 | bytes 6905463 | solution.py:111
  106.3 8.5 gather_fusion
  122.9 8.5 gather_fusion
  139.5 8.5 gather_fusion
  156.1 8.5 gather_fusion
  165.9 8.9 %while.107 = (s32[]{:T(128)}, f32[512]{0:T(512)S(1)}, f32[512]{0:T(512)S(1)}, s32[]{:T(128)}, s32[3]{0:T(128)S(1)}, /*index=5*/f32[20480,256]{1,0:T(8,128)}, f32...) while((s32[]{:T(128)}, f32[512]{0:T(512)S(1)}, ...), condition=%wide.region_4.4_spmd, body=%wide.region_1.3_spmd.sunk | while | flops 806093824 | bytes 3172573 | solution.py:57
  176.8 8.5 gather_fusion
  186.6 8.9 %while.107 = (s32[]{:T(128)}, f32[512]{0:T(512)S(1)}, f32[512]{0:T(512)S(1)}, s32[]{:T(128)}, s32[3]{0:T(128)S(1)}, /*index=5*/f32[20480,256]{1,0:T(8,128)}, f32...) while((s32[]{:T(128)}, f32[512]{0:T(512)S(1)}, ...), condition=%wide.region_4.4_spmd, body=%wide.region_1.3_spmd.sunk | while | flops 806093824 | bytes 3172573 | solution.py:57
  197.5 8.5 gather_fusion
  207.3 8.9 %while.107 = (s32[]{:T(128)}, f32[512]{0:T(512)S(1)}, f32[512]{0:T(512)S(1)}, s32[]{:T(128)}, s32[3]{0:T(128)S(1)}, /*index=5*/f32[20480,256]{1,0:T(8,128)}, f32...) while((s32[]{:T(128)}, f32[512]{0:T(512)S(1)}, ...), condition=%wide.region_4.4_spmd, body=%wide.region_1.3_spmd.sunk | while | flops 806093824 | bytes 3172573 | solution.py:57
  218.2 8.5 gather_fusion
  228.0 8.9 %while.107 = (s32[]{:T(128)}, f32[512]{0:T(512)S(1)}, f32[512]{0:T(512)S(1)}, s32[]{:T(128)}, s32[3]{0:T(128)S(1)}, /*index=5*/f32[20480,256]{1,0:T(8,128)}, f32...) while((s32[]{:T(128)}, f32[512]{0:T(512)S(1)}, ...), condition=%wide.region_4.4_spmd, body=%wide.region_1.3_spmd.sunk | while | flops 806093824 | bytes 3172573 | solution.py:57
  248.7 13.0 %while.107 = (s32[]{:T(128)}, f32[512]{0:T(512)S(1)}, f32[512]{0:T(512)S(1)}, s32[]{:T(128)}, s32[3]{0:T(128)S(1)}, /*index=5*/f32[20480,256]{1,0:T(8,128)}, f32...) while((s32[]{:T(128)}, f32[512]{0:T(512)S(1)}, ...), condition=%wide.region_4.4_spmd, body=%wide.region_1.3_spmd.sunk | while | flops 806093824 | bytes 3172573 | solution.py:57
  262.9 37.4 %all-gather = f32[64,512]{1,0:T(8,128)S(1)} all-gather(f32[8,512]{1,0:T(8,128)S(1)} %get-tuple-element.572), channel_id=2, replica_groups=mesh['dp'=16,'shard'=8] {'shard'}, dimensions={0}, use_global_device_ids=true | all-gather | bytes 147456 | tf_op jit(solution)/shard_map/all_gather | solution.py:13
  300.3 21.8 %all-gather.1 = f32[64,512]{1,0:T(8,128)S(1)} all-gather(f32[8,512]{1,0:T(8,128)S(1)} %get-tuple-element.573), channel_id=3, replica_groups=mesh['dp'=16,'shard'=8] {'shard'}, dimensions={0}, use_global_device_ids=true | all-gather | bytes 147456 | tf_op jit(solution)/shard_map/all_gather | solution.py:13
  322.1 21.8 %all-gather.2 = f32[64,512]{1,0:T(8,128)S(1)} all-gather(f32[8,512]{1,0:T(8,128)S(1)} %get-tuple-element.1349), channel_id=4, replica_groups=mesh['dp'=16,'shard'=8] {'shard'}, dimensions={0}, use_global_device_ids=true | all-gather | bytes 147456 | tf_op jit(solution)/shard_map/all_gather | solution.py:13
  356.2 180.7 %while.106 = (s32[]{:T(128)}, f32[20480,256]{1,0:T(8,128)}, f32[8,512,256]{2,1,0:T(8,128)}, f32[8,512,256]{2,1,0:T(8,128)}, s32[8]{0:T(128)S(1)}, /*index=5*/s32...) while((s32[]{:T(128)}, f32[20480,256]{1,0:T(8,128)}, ...), condition=%wide.region_12.14_spmd, body=%wide.region_9.13_spmd.sunk | while | flops 2416838144 | bytes 11032662 | solution.py:126
  358.9 10.5 %while.108 = (s32[]{:T(128)}, f32[512,256]{1,0:T(8,128)S(1)}, f32[20480,256]{1,0:T(8,128)}, s32[]{:T(128)}, s32[3]{0:T(128)S(1)}, /*index=5*/f32[20480,256]{1,0:...) while((s32[]{:T(128)}, f32[512,256]{1,0:T(8,128)S(1)}, ...), condition=%wide.region_11.12_spmd, body=%wide.region_10.11_spmd.sunk | while | flops 2416443392 | bytes 7342317 | solution.py:80
  374.1 10.5 %while.108 = (s32[]{:T(128)}, f32[512,256]{1,0:T(8,128)S(1)}, f32[20480,256]{1,0:T(8,128)}, s32[]{:T(128)}, s32[3]{0:T(128)S(1)}, /*index=5*/f32[20480,256]{1,0:...) while((s32[]{:T(128)}, f32[512,256]{1,0:T(8,128)S(1)}, ...), condition=%wide.region_11.12_spmd, body=%wide.region_10.11_spmd.sunk | while | flops 2416443392 | bytes 7342317 | solution.py:80
  389.4 10.5 %while.108 = (s32[]{:T(128)}, f32[512,256]{1,0:T(8,128)S(1)}, f32[20480,256]{1,0:T(8,128)}, s32[]{:T(128)}, s32[3]{0:T(128)S(1)}, /*index=5*/f32[20480,256]{1,0:...) while((s32[]{:T(128)}, f32[512,256]{1,0:T(8,128)S(1)}, ...), condition=%wide.region_11.12_spmd, body=%wide.region_10.11_spmd.sunk | while | flops 2416443392 | bytes 7342317 | solution.py:80
  404.5 20.4 %while.108 = (s32[]{:T(128)}, f32[512,256]{1,0:T(8,128)S(1)}, f32[20480,256]{1,0:T(8,128)}, s32[]{:T(128)}, s32[3]{0:T(128)S(1)}, /*index=5*/f32[20480,256]{1,0:...) while((s32[]{:T(128)}, f32[512,256]{1,0:T(8,128)S(1)}, ...), condition=%wide.region_11.12_spmd, body=%wide.region_10.11_spmd.sunk | while | flops 2416443392 | bytes 7342317 | solution.py:80
  429.6 20.4 %while.108 = (s32[]{:T(128)}, f32[512,256]{1,0:T(8,128)S(1)}, f32[20480,256]{1,0:T(8,128)}, s32[]{:T(128)}, s32[3]{0:T(128)S(1)}, /*index=5*/f32[20480,256]{1,0:...) while((s32[]{:T(128)}, f32[512,256]{1,0:T(8,128)S(1)}, ...), condition=%wide.region_11.12_spmd, body=%wide.region_10.11_spmd.sunk | while | flops 2416443392 | bytes 7342317 | solution.py:80
  454.6 20.4 %while.108 = (s32[]{:T(128)}, f32[512,256]{1,0:T(8,128)S(1)}, f32[20480,256]{1,0:T(8,128)}, s32[]{:T(128)}, s32[3]{0:T(128)S(1)}, /*index=5*/f32[20480,256]{1,0:...) while((s32[]{:T(128)}, f32[512,256]{1,0:T(8,128)S(1)}, ...), condition=%wide.region_11.12_spmd, body=%wide.region_10.11_spmd.sunk | while | flops 2416443392 | bytes 7342317 | solution.py:80
  479.6 20.4 %while.108 = (s32[]{:T(128)}, f32[512,256]{1,0:T(8,128)S(1)}, f32[20480,256]{1,0:T(8,128)}, s32[]{:T(128)}, s32[3]{0:T(128)S(1)}, /*index=5*/f32[20480,256]{1,0:...) while((s32[]{:T(128)}, f32[512,256]{1,0:T(8,128)S(1)}, ...), condition=%wide.region_11.12_spmd, body=%wide.region_10.11_spmd.sunk | while | flops 2416443392 | bytes 7342317 | solution.py:80
  504.7 30.2 %while.108 = (s32[]{:T(128)}, f32[512,256]{1,0:T(8,128)S(1)}, f32[20480,256]{1,0:T(8,128)}, s32[]{:T(128)}, s32[3]{0:T(128)S(1)}, /*index=5*/f32[20480,256]{1,0:...) while((s32[]{:T(128)}, f32[512,256]{1,0:T(8,128)S(1)}, ...), condition=%wide.region_11.12_spmd, body=%wide.region_10.11_spmd.sunk | while | flops 2416443392 | bytes 7342317 | solution.py:80
  537.2 36.7 %scatter_fusion = f32[20480,256]{1,0:T(8,128)} fusion(f32[20480,256]{1,0:T(8,128)} %get-tuple-element.581, s32[4096]{0:T(1024)S(1)} %bitcast.132, f32[4096,256]{1,0:T(8,128)} %bitcast.118), kind=kCustom, calls=%fused_computation.1 | custom fusion | flops 1048576 | bytes 12599296 | tf_op jit(solution)/shard_map/scatter-add | solution.py:129
  574.6 121.9 %reduce-scatter.3.cloned.1.call-done = f32[1,512,256]{2,1,0:T(8,128)} async-done(((f32[8,512,256]{2,1,0:T(8,128)}), f32[1,512,256]{2,1,0:T(8,128)}) %reduce-scatter.3.cloned.1.call-update) | async-done | bytes 524304 | tf_op jit(solution)/shard_map/reduce_scatter | solution.py:130
  696.4 173.5 %reduce-scatter.5.cloned.1.call-done = f32[1280,256]{1,0:T(8,128)} async-done(((f32[20480,256]{1,0:T(8,128)}), f32[1280,256]{1,0:T(8,128)}) %reduce-scatter.5.cloned.1.call-update) | async-done | bytes 1310736 | tf_op jit(solution)/shard_map/reduce_scatter | solution.py:133
  (389 shorter events, 263.0 us)
Async XLA Ops:
  7.2 96.0 %all-gather.7.cloned.1.call-start = ((), (), s32[]{:S(2)}) async-start(), calls=%async_computation.2 | async-start | bytes 4718592 | tf_op jit(solution)/shard_map/all_gather | solution.py:98
  7.9 688.5 %reduce-scatter.3.cloned.1.call-start = ((), (), s32[]{:S(2)}) async-start(), calls=%async_computation.3 | async-start | bytes 4718592 | tf_op jit(solution)/shard_map/reduce_scatter | solution.py:130
  536.9 333.0 %reduce-scatter.5.cloned.1.call-start = ((), (), s32[]{:S(2)}) async-start(), calls=%async_computation.4 | async-start | bytes 22282240 | tf_op jit(solution)/shard_map/reduce_scatter | solution.py:133
Sparse Core Ops, SparseCore 0:
  9.6 93.4 all-gather.6
  537.0 159.3 reduce-scatter.2
  701.4 168.5 reduce-scatter.4
where the time goes:
time: 883 us; the launch traced here: 876 us
  waiting for transfers between devices  327 us (37%)
  blocking collectives  144 us (16%)
  matrix products  140 us (16%)
  local copies, waits for them, and re-layouts  112 us (13%)
  other arithmetic  91.4 us (10%)
  loops' own time  47.4 us (5%)
  between operations  13.8 us (2%)
    reduce_scatter x1, waiting for transfers between devices, local(): item_grad = lax.psum_scatter(d_local, 'dp', scatter_dimension=0, tiled=True)  174 us
    reduce_scatter x1, waiting for transfers between devices, local(): lax.psum_scatter(dq_parts, 'shard', scatter_dimension=0, tiled=True)  122 us
    all_gather x3, blocking collectives, joined(): gathered = jax.tree.map(lambda a: lax.all_gather(a, axis), part)  81.1 us
    gather x8, local copies, waits for them, and re-layouts, positive_row(): chosen = jnp.take(items, safe, axis=0)  68.3 us
    dot_general x28, matrix products, tile_logits(): jnp.einsum('qd,td->qt', qblk, block, precision=lax.Precision.HIGHEST, pre...  58.9 us
    dot_general x14, matrix products, visit(): jnp.dot(prob, block, precision=high, preferred_element_type=jnp.float32)  41.6 us
    dot_general x14, matrix products, visit(): jnp.einsum('qt,qd->td', prob, qblk, precision=high, preferred_element_typ...  39.8 us
    dynamic_update_slice x24, other arithmetic, local(): lax.map(stats_of, (seen_q, seen_pos, idrows, seen_counts))  39.5 us
  transfers between devices with their start and end apart: 3, of which 3 were waited for; matrix products, arithmetic and copies ran while one was open for 4% of the time, Pallas kernels for 0%

commit v1 on v0

--- a/solution.py
+++ b/solution.py
@@ -89,19 +89,31 @@
     return (top, total, first[2] + second[2])
 
 
+def gather_packed(queries, positive, tile_ids, counts):
+    rows, width = queries.shape
+    n_shard = lax.axis_size("shard")
+    pos_rows = rows // width
+    ints = jnp.concatenate([tile_ids.reshape(-1), counts.reshape(-1)]).astype(jnp.float32)
+    extra = jnp.zeros((8, width), jnp.float32)
+    extra = extra.at[:pos_rows].set(positive.astype(jnp.float32).reshape(pos_rows, width))
+    extra = extra.at[pos_rows, : ints.shape[0]].set(ints)
+    packed = jnp.concatenate([queries, extra], axis=0)
+    seen = lax.all_gather(packed, "shard")
+    seen_q = seen[:, :rows]
+    seen_pos = seen[:, rows : rows + pos_rows].reshape(n_shard, rows).astype(jnp.int32)
+    n_ids = tile_ids.size
+    flat = seen[:, rows + pos_rows].astype(jnp.int32)
+    seen_ids = flat[:, :n_ids].reshape((n_shard,) + tile_ids.shape[1:])
+    seen_cnt = flat[:, n_ids : n_ids + counts.size].reshape((n_shard,) + counts.shape[1:])
+    return seen_q, seen_pos, seen_ids, seen_cnt
+
+
 def local(queries, items, positive, tile_ids, counts):
     shard_at = lax.axis_index("shard")
     n_shard = lax.axis_size("shard")
     rows = queries.shape[0]
     width = queries.shape[1]
-    seen_q, seen_pos, seen_ids, seen_cnt = (
-        lax.all_gather(queries, "shard", axis=0, tiled=True),
-        lax.all_gather(positive, "shard", axis=0, tiled=True),
-        lax.all_gather(tile_ids, "shard", axis=0, tiled=True),
-        lax.all_gather(counts, "shard", axis=0, tiled=True),
-    )
-    seen_q = seen_q.reshape(n_shard, rows, width)
-    seen_pos = seen_pos.reshape(n_shard, rows)
+    seen_q, seen_pos, seen_ids, seen_cnt = gather_packed(queries, positive, tile_ids, counts)
     idrows = jnp.take(seen_ids, shard_at, axis=1)
     seen_counts = jnp.take(seen_cnt, shard_at, axis=1)
 
@@ -112,7 +124,13 @@
         stats_of, (seen_q, seen_pos, idrows, seen_counts)
     )
     local_plogs = plogs
-    tops, totals, plogs = joined((tops, totals, plogs), "shard", combine_stats)
+    stacked = lax.all_gather(jnp.stack([tops, totals, plogs]), "shard")
+    tops, totals, plogs = lax.fori_loop(
+        1,
+        n_shard,
+        lambda source, state: combine_stats(state, tuple(stacked[source])),
+        tuple(stacked[0]),
+    )
     lse = tops + jnp.log(totals)
     loss = jnp.take(lse, shard_at, axis=0) - jnp.take(plogs, shard_at, axis=0)
     d_local = jnp.zeros(items.shape, jnp.float32)

time: 883 us -> 815 us (0.923)
  blocking collectives: 144 us -> 30.1 us
  waiting for transfers between devices: 327 us -> 363 us
    all_gather x6 -> x1, blocking collectives: 144 us -> 30.1 us  [local(): stacked = lax.all_gather(jnp.stack([tops, totals, plogs]), 'shard')]
    all_gather x1, waiting for transfers between devices: 31.3 us -> 94.2 us  [gather_packed(): seen = lax.all_gather(packed, 'shard')]
    reduce_scatter x1, waiting for transfers between devices: 122 us -> 95.4 us  [local(): lax.psum_scatter(dq_parts, 'shard', scatter_dimension=0, tiled=True)]
  transfers between devices with their start and end apart: 3 -> 3, of which waited for: 3 -> 3; matrix products, arithmetic and copies ran while one was open for 4% -> 5% of each run, Pallas kernels for 0% -> 0%
where the time goes in v1:
time: 815 us; the launch traced here: 809 us
  waiting for transfers between devices  363 us (45%)
  matrix products  140 us (17%)
  local copies, waits for them, and re-layouts  117 us (14%)
  other arithmetic  96.2 us (12%)
  loops' own time  47 us (6%)
  blocking collectives  30.1 us (4%)
  between operations  13.9 us (2%)
    reduce_scatter x1, waiting for transfers between devices, local(): item_grad = lax.psum_scatter(d_local, 'dp', scatter_dimension=0, tiled=True)  174 us
    reduce_scatter x1, waiting for transfers between devices, local(): lax.psum_scatter(dq_parts, 'shard', scatter_dimension=0, tiled=True)  95.4 us
    all_gather x1, waiting for transfers between devices, gather_packed(): seen = lax.all_gather(packed, 'shard')  94.2 us
    gather x8, local copies, waits for them, and re-layouts, positive_row(): chosen = jnp.take(items, safe, axis=0)  68.3 us
    dot_general x28, matrix products, tile_logits(): jnp.einsum('qd,td->qt', qblk, block, precision=lax.Precision.HIGHEST, pre...  58.9 us
    dot_general x14, matrix products, visit(): jnp.dot(prob, block, precision=high, preferred_element_type=jnp.float32)  41.6 us
    dot_general x14, matrix products, visit(): jnp.einsum('qt,qd->td', prob, qblk, precision=high, preferred_element_typ...  39.7 us
    dynamic_update_slice x24, other arithmetic, local(): lax.map(stats_of, (seen_q, seen_pos, idrows, seen_counts))  39.5 us
  transfers between devices with their start and end apart: 3, of which 3 were waited for; matrix products, arithmetic and copies ran while one was open for 5% of the time, Pallas kernels for 0%

profile of v1, /device:TPU:1, one launch (start us, length us, event | category | flops | bytes accessed | tf_op | source)
XLA Modules:
  0.0 808.5 jit_solution(1549498688255933902)
XLA Ops:
  11.7 94.2 %all-gather.4.cloned.1.call-done = f32[4160,256]{1,0:T(8,128)} async-done(((f32[520,256]{1,0:T(8,128)}), f32[4160,256]{1,0:T(8,128)}) %all-gather.4.cloned.1.call-update) | async-done | bytes 4259856 | tf_op jit(solution)/shard_map/all_gather | solution.py:101
  114.9 157.2 %while.105 = (s32[]{:T(128)}, f32[8,512]{1,0:T(8,128)S(1)}, f32[8,512]{1,0:T(8,128)S(1)}, f32[8,512]{1,0:T(8,128)S(1)}, pred[8,512]{1,0:T(8,128)(4,1)S(1)}, /*in...) while((s32[]{:T(128)}, f32[8,512]{1,0:T(8,128)S(1)}, ...), condition=%wide.region_6.7_spmd, body=%wide.region_0.6_spmd.sunk | while | flops 806631936 | bytes 6905463 | solution.py:123
  115.7 8.5 %gather_fusion = f32[512,256]{1,0:T(8,128)S(1)} fusion(f32[20480,256]{1,0:T(8,128)} %get-tuple-element.1263, s32[1024]{0:T(1024)S(1)} %pad_clamp_fusion.2), kind=kCustom, calls=%fused_computation.clone.1 | custom fusion | bytes 1050624 | tf_op jit(solution)/shard_map/while/body/eval_jaxpr/jit(_take)/gather | solution.py:29
  125.5 8.9 %while.109 = (s32[]{:T(128)}, f32[512]{0:T(512)S(1)}, f32[512]{0:T(512)S(1)}, s32[]{:T(128)}, s32[3]{0:T(128)S(1)}, /*index=5*/f32[20480,256]{1,0:T(8,128)}, f32...) while((s32[]{:T(128)}, f32[512]{0:T(512)S(1)}, ...), condition=%wide.region_4.4_spmd, body=%wide.region_1.3_spmd.sunk | while | flops 806093824 | bytes 3172573 | solution.py:57
  136.4 8.5 %gather_fusion = f32[512,256]{1,0:T(8,128)S(1)} fusion(f32[20480,256]{1,0:T(8,128)} %get-tuple-element.1263, s32[1024]{0:T(1024)S(1)} %pad_clamp_fusion.2), kind=kCustom, calls=%fused_computation.clone.1 | custom fusion | bytes 1050624 | tf_op jit(solution)/shard_map/while/body/eval_jaxpr/jit(_take)/gather | solution.py:29
  146.2 4.7 while.109
  152.9 8.5 %gather_fusion = f32[512,256]{1,0:T(8,128)S(1)} fusion(f32[20480,256]{1,0:T(8,128)} %get-tuple-element.1263, s32[1024]{0:T(1024)S(1)} %pad_clamp_fusion.2), kind=kCustom, calls=%fused_computation.clone.1 | custom fusion | bytes 1050624 | tf_op jit(solution)/shard_map/while/body/eval_jaxpr/jit(_take)/gather | solution.py:29
  162.8 8.9 %while.109 = (s32[]{:T(128)}, f32[512]{0:T(512)S(1)}, f32[512]{0:T(512)S(1)}, s32[]{:T(128)}, s32[3]{0:T(128)S(1)}, /*index=5*/f32[20480,256]{1,0:T(8,128)}, f32...) while((s32[]{:T(128)}, f32[512]{0:T(512)S(1)}, ...), condition=%wide.region_4.4_spmd, body=%wide.region_1.3_spmd.sunk | while | flops 806093824 | bytes 3172573 | solution.py:57
  173.6 8.5 %gather_fusion = f32[512,256]{1,0:T(8,128)S(1)} fusion(f32[20480,256]{1,0:T(8,128)} %get-tuple-element.1263, s32[1024]{0:T(1024)S(1)} %pad_clamp_fusion.2), kind=kCustom, calls=%fused_computation.clone.1 | custom fusion | bytes 1050624 | tf_op jit(solution)/shard_map/while/body/eval_jaxpr/jit(_take)/gather | solution.py:29
  183.5 8.9 %while.109 = (s32[]{:T(128)}, f32[512]{0:T(512)S(1)}, f32[512]{0:T(512)S(1)}, s32[]{:T(128)}, s32[3]{0:T(128)S(1)}, /*index=5*/f32[20480,256]{1,0:T(8,128)}, f32...) while((s32[]{:T(128)}, f32[512]{0:T(512)S(1)}, ...), condition=%wide.region_4.4_spmd, body=%wide.region_1.3_spmd.sunk | while | flops 806093824 | bytes 3172573 | solution.py:57
  194.3 8.5 %gather_fusion = f32[512,256]{1,0:T(8,128)S(1)} fusion(f32[20480,256]{1,0:T(8,128)} %get-tuple-element.1263, s32[1024]{0:T(1024)S(1)} %pad_clamp_fusion.2), kind=kCustom, calls=%fused_computation.clone.1 | custom fusion | bytes 1050624 | tf_op jit(solution)/shard_map/while/body/eval_jaxpr/jit(_take)/gather | solution.py:29
  204.1 8.9 %while.109 = (s32[]{:T(128)}, f32[512]{0:T(512)S(1)}, f32[512]{0:T(512)S(1)}, s32[]{:T(128)}, s32[3]{0:T(128)S(1)}, /*index=5*/f32[20480,256]{1,0:T(8,128)}, f32...) while((s32[]{:T(128)}, f32[512]{0:T(512)S(1)}, ...), condition=%wide.region_4.4_spmd, body=%wide.region_1.3_spmd.sunk | while | flops 806093824 | bytes 3172573 | solution.py:57
  215.0 8.5 %gather_fusion = f32[512,256]{1,0:T(8,128)S(1)} fusion(f32[20480,256]{1,0:T(8,128)} %get-tuple-element.1263, s32[1024]{0:T(1024)S(1)} %pad_clamp_fusion.2), kind=kCustom, calls=%fused_computation.clone.1 | custom fusion | bytes 1050624 | tf_op jit(solution)/shard_map/while/body/eval_jaxpr/jit(_take)/gather | solution.py:29
  224.8 4.7 while.109
  231.5 8.5 %gather_fusion = f32[512,256]{1,0:T(8,128)S(1)} fusion(f32[20480,256]{1,0:T(8,128)} %get-tuple-element.1263, s32[1024]{0:T(1024)S(1)} %pad_clamp_fusion.2), kind=kCustom, calls=%fused_computation.clone.1 | custom fusion | bytes 1050624 | tf_op jit(solution)/shard_map/while/body/eval_jaxpr/jit(_take)/gather | solution.py:29
  241.4 4.7 while.109
  248.0 8.5 %gather_fusion = f32[512,256]{1,0:T(8,128)S(1)} fusion(f32[20480,256]{1,0:T(8,128)} %get-tuple-element.1263, s32[1024]{0:T(1024)S(1)} %pad_clamp_fusion.2), kind=kCustom, calls=%fused_computation.clone.1 | custom fusion | bytes 1050624 | tf_op jit(solution)/shard_map/while/body/eval_jaxpr/jit(_take)/gather | solution.py:29
  257.9 13.0 %while.109 = (s32[]{:T(128)}, f32[512]{0:T(512)S(1)}, f32[512]{0:T(512)S(1)}, s32[]{:T(128)}, s32[3]{0:T(128)S(1)}, /*index=5*/f32[20480,256]{1,0:T(8,128)}, f32...) while((s32[]{:T(128)}, f32[512]{0:T(512)S(1)}, ...), condition=%wide.region_4.4_spmd, body=%wide.region_1.3_spmd.sunk | while | flops 806093824 | bytes 3172573 | solution.py:57
  272.1 30.1 %all-gather.1 = f32[24,8,512]{2,1,0:T(8,128)S(1)} all-gather(f32[3,8,512]{2,1,0:T(8,128)S(1)} %pad_maximum_fusion.1), channel_id=3, replica_groups=mesh['dp'=16,'shard'=8] {'shard'}, dimensions={0}, use_global_device_ids=true | all-gather | bytes 442368 | tf_op jit(solution)/shard_map/all_gather | solution.py:127
  307.2 7.2 broadcast_in_dim.95
  314.4 180.7 %while.108 = (s32[]{:T(128)}, f32[20480,256]{1,0:T(8,128)}, f32[8,512,256]{2,1,0:T(8,128)}, f32[8,512,256]{2,1,0:T(8,128)}, s32[8]{0:T(128)S(1)}, /*index=5*/s32...) while((s32[]{:T(128)}, f32[20480,256]{1,0:T(8,128)}, ...), condition=%wide.region_12.14_spmd, body=%wide.region_9.13_spmd.sunk | while | flops 2416838144 | bytes 11032662 | solution.py:144
  317.1 20.4 %while.110 = (s32[]{:T(128)}, f32[512,256]{1,0:T(8,128)S(1)}, f32[20480,256]{1,0:T(8,128)}, s32[]{:T(128)}, s32[3]{0:T(128)S(1)}, /*index=5*/f32[20480,256]{1,0:...) while((s32[]{:T(128)}, f32[512,256]{1,0:T(8,128)S(1)}, ...), condition=%wide.region_11.12_spmd, body=%wide.region_10.11_spmd.sunk | while | flops 2416443392 | bytes 7342317 | solution.py:80
  342.2 10.5 %while.110 = (s32[]{:T(128)}, f32[512,256]{1,0:T(8,128)S(1)}, f32[20480,256]{1,0:T(8,128)}, s32[]{:T(128)}, s32[3]{0:T(128)S(1)}, /*index=5*/f32[20480,256]{1,0:...) while((s32[]{:T(128)}, f32[512,256]{1,0:T(8,128)S(1)}, ...), condition=%wide.region_11.12_spmd, body=%wide.region_10.11_spmd.sunk | while | flops 2416443392 | bytes 7342317 | solution.py:80
  357.5 20.4 %while.110 = (s32[]{:T(128)}, f32[512,256]{1,0:T(8,128)S(1)}, f32[20480,256]{1,0:T(8,128)}, s32[]{:T(128)}, s32[3]{0:T(128)S(1)}, /*index=5*/f32[20480,256]{1,0:...) while((s32[]{:T(128)}, f32[512,256]{1,0:T(8,128)S(1)}, ...), condition=%wide.region_11.12_spmd, body=%wide.region_10.11_spmd.sunk | while | flops 2416443392 | bytes 7342317 | solution.py:80
  382.5 20.4 %while.110 = (s32[]{:T(128)}, f32[512,256]{1,0:T(8,128)S(1)}, f32[20480,256]{1,0:T(8,128)}, s32[]{:T(128)}, s32[3]{0:T(128)S(1)}, /*index=5*/f32[20480,256]{1,0:...) while((s32[]{:T(128)}, f32[512,256]{1,0:T(8,128)S(1)}, ...), condition=%wide.region_11.12_spmd, body=%wide.region_10.11_spmd.sunk | while | flops 2416443392 | bytes 7342317 | solution.py:80
  407.5 20.3 %while.110 = (s32[]{:T(128)}, f32[512,256]{1,0:T(8,128)S(1)}, f32[20480,256]{1,0:T(8,128)}, s32[]{:T(128)}, s32[3]{0:T(128)S(1)}, /*index=5*/f32[20480,256]{1,0:...) while((s32[]{:T(128)}, f32[512,256]{1,0:T(8,128)S(1)}, ...), condition=%wide.region_11.12_spmd, body=%wide.region_10.11_spmd.sunk | while | flops 2416443392 | bytes 7342317 | solution.py:80
  432.5 10.5 %while.110 = (s32[]{:T(128)}, f32[512,256]{1,0:T(8,128)S(1)}, f32[20480,256]{1,0:T(8,128)}, s32[]{:T(128)}, s32[3]{0:T(128)S(1)}, /*index=5*/f32[20480,256]{1,0:...) while((s32[]{:T(128)}, f32[512,256]{1,0:T(8,128)S(1)}, ...), condition=%wide.region_11.12_spmd, body=%wide.region_10.11_spmd.sunk | while | flops 2416443392 | bytes 7342317 | solution.py:80
  447.7 10.5 %while.110 = (s32[]{:T(128)}, f32[512,256]{1,0:T(8,128)S(1)}, f32[20480,256]{1,0:T(8,128)}, s32[]{:T(128)}, s32[3]{0:T(128)S(1)}, /*index=5*/f32[20480,256]{1,0:...) while((s32[]{:T(128)}, f32[512,256]{1,0:T(8,128)S(1)}, ...), condition=%wide.region_11.12_spmd, body=%wide.region_10.11_spmd.sunk | while | flops 2416443392 | bytes 7342317 | solution.py:80
  462.9 30.2 %while.110 = (s32[]{:T(128)}, f32[512,256]{1,0:T(8,128)S(1)}, f32[20480,256]{1,0:T(8,128)}, s32[]{:T(128)}, s32[3]{0:T(128)S(1)}, /*index=5*/f32[20480,256]{1,0:...) while((s32[]{:T(128)}, f32[512,256]{1,0:T(8,128)S(1)}, ...), condition=%wide.region_11.12_spmd, body=%wide.region_10.11_spmd.sunk | while | flops 2416443392 | bytes 7342317 | solution.py:80
  495.4 36.7 %scatter_fusion = f32[20480,256]{1,0:T(8,128)} fusion(f32[20480,256]{1,0:T(8,128)} %get-tuple-element.561, s32[4096]{0:T(1024)S(1)} %bitcast.147, f32[4096,256]{1,0:T(8,128)} %bitcast.132), kind=kCustom, calls=%fused_computation.1 | custom fusion | flops 1048576 | bytes 12599296 | tf_op jit(solution)/shard_map/scatter-add | solution.py:147
  532.8 95.4 %reduce-scatter.3.cloned.1.call-done = f32[1,512,256]{2,1,0:T(8,128)} async-done(((f32[8,512,256]{2,1,0:T(8,128)}), f32[1,512,256]{2,1,0:T(8,128)}) %reduce-scatter.3.cloned.1.call-update) | async-done | bytes 524304 | tf_op jit(solution)/shard_map/reduce_scatter | solution.py:148
  628.1 173.9 %reduce-scatter.5.cloned.1.call-done = f32[1280,256]{1,0:T(8,128)} async-done(((f32[20480,256]{1,0:T(8,128)}), f32[1280,256]{1,0:T(8,128)}) %reduce-scatter.5.cloned.1.call-update) | async-done | bytes 1310736 | tf_op jit(solution)/shard_map/reduce_scatter | solution.py:151
  (397 shorter events, 242.2 us)
Async XLA Ops:
  7.2 98.7 %all-gather.4.cloned.1.call-start = ((), (), s32[]{:S(2)}) async-start(), calls=%async_computation.4 | async-start | bytes 4792320 | tf_op jit(solution)/shard_map/all_gather | solution.py:101
  11.6 616.6 %reduce-scatter.3.cloned.1.call-start = ((), (), s32[]{:S(2)}) async-start(), calls=%async_computation.2 | async-start | bytes 4718592 | tf_op jit(solution)/shard_map/reduce_scatter | solution.py:148
  495.1 306.9 %reduce-scatter.5.cloned.1.call-start = ((), (), s32[]{:S(2)}) async-start(), calls=%async_computation.3 | async-start | bytes 22282240 | tf_op jit(solution)/shard_map/reduce_scatter | solution.py:151
Sparse Core Ops, SparseCore 0:
  11.7 94.1 all-gather.3
  495.2 132.8 reduce-scatter.2
  633.1 168.8 reduce-scatter.4

commit v2 on v1

v2 whole, which is shorter than its diff:
```python
import functools

import jax
import jax.numpy as jnp
from jax import lax
from jax.experimental import pallas as pl
from jax.experimental.pallas import tpu as pltpu
from jax.sharding import PartitionSpec as P

TILE = 512
KMAX = 3

very_low = -1e30
BF = jnp.bfloat16
F32 = jnp.float32


def split(x):
    hi = x.astype(BF)
    return hi, (x - hi.astype(F32)).astype(BF)


def mm(a, b, ca, cb):
    return lax.dot_general(a, b, (((ca,), (cb,)), ((), ())), preferred_element_type=F32)


def mm3(ah, al, bh, bl, ca, cb):
    return mm(ah, bh, ca, cb) + mm(ah, bl, ca, cb) + mm(al, bh, ca, cb)


def stats_kernel(ids_ref, cnt_ref, q_ref, t_ref, m_out, l_out, dq_out, qh_s, ql_s, m_s, l_s, dq_s):
    j = pl.program_id(0)
    k = pl.program_id(1)

    @pl.when(k == 0)
    def _():
        qh, ql = split(q_ref[0])
        qh_s[...] = qh
        ql_s[...] = ql
        m_s[...] = jnp.full(m_s.shape, very_low, F32)
        l_s[...] = jnp.zeros(l_s.shape, F32)
        dq_s[...] = jnp.zeros(dq_s.shape, F32)

    @pl.when(k < cnt_ref[j])
    def _():
        th, tl = split(t_ref[...])
        logits = mm3(qh_s[...], ql_s[...], th, tl, 1, 1)
        m_old = m_s[...]
        m_new = jnp.maximum(m_old, jnp.max(logits, axis=1, keepdims=True))
        alpha = jnp.exp(m_old - m_new)
        prob = jnp.exp(logits - m_new)
        l_s[...] = alpha * l_s[...] + jnp.sum(prob, axis=1, keepdims=True)
        ph, plo = split(prob)
        dq_s[...] = alpha * dq_s[...] + mm3(ph, plo, th, tl, 1, 0)
        m_s[...] = m_new

    @pl.when(k == KMAX - 1)
    def _():
        m_out[0] = m_s[...]
        l_out[0] = l_s[...]
        dq_out[0] = dq_s[...]


def block_stats(seen_q, items, ids_flat, cnt):
    nb, rows, width = seen_q.shape

    def tile_map(j, k, ids, cnt):
        return (ids[j * KMAX + jnp.minimum(k, cnt[j] - 1)], 0)

    return pl.pallas_call(
        stats_kernel,
        out_shape=(
            jax.ShapeDtypeStruct((nb, rows, 1), F32),
            jax.ShapeDtypeStruct((nb, rows, 1), F32),
            jax.ShapeDtypeStruct((nb, rows, width), F32),
        ),
        grid_spec=pltpu.PrefetchScalarGridSpec(
            num_scalar_prefetch=2,
            grid=(nb, KMAX),
            in_specs=[
                pl.BlockSpec((1, rows, width), lambda j, k, ids, cnt: (j, 0, 0)),
                pl.BlockSpec((TILE, width), tile_map),
            ],
            out_specs=[
                pl.BlockSpec((1, rows, 1), lambda j, k, ids, cnt: (j, 0, 0)),
                pl.BlockSpec((1, rows, 1), lambda j, k, ids, cnt: (j, 0, 0)),
                pl.BlockSpec((1, rows, width), lambda j, k, ids, cnt: (j, 0, 0)),
            ],
            scratch_shapes=[
                pltpu.VMEM((rows, width), BF),
                pltpu.VMEM((rows, width), BF),
                pltpu.VMEM((rows, 1), F32),
                pltpu.VMEM((rows, 1), F32),
                pltpu.VMEM((rows, width), F32),
            ],
        ),
        compiler_params=pltpu.CompilerParams(dimension_semantics=("arbitrary", "arbitrary")),
        cost_estimate=pl.CostEstimate(
            flops=nb * KMAX * 6 * 2 * rows * TILE * width,
            transcendentals=nb * KMAX * rows * TILE,
            bytes_accessed=nb * (KMAX + 2) * rows * width * 4,
        ),
    )(ids_flat, cnt, seen_q, items)


def grads_kernel(ids_ref, cnt_ref, acc_ref, t_ref, q_ref, lse_ref, out_ref):
    t = pl.program_id(0)
    th, tl = split(t_ref[...])
    out_ref[...] = acc_ref[...]
    nb = q_ref.shape[0]

    def visit(v, carry):
        j = v // KMAX
        k = v % KMAX

        @pl.when((k < cnt_ref[j]) & (ids_ref[v] == t))
        def _():
            qh, ql = split(q_ref[j])
            logits_t = mm3(th, tl, qh, ql, 1, 1)
            prob_t = jnp.exp(logits_t - lse_ref[j])
            ph, plo = split(prob_t)
            out_ref[...] += mm3(ph, plo, qh, ql, 1, 0)

        return carry

    lax.fori_loop(0, nb * KMAX, visit, 0)


def tile_grads(acc, items, seen_q, lse, ids_flat, cnt):
    n_rows, width = items.shape
    nb, rows, _ = seen_q.shape
    n_tiles = n_rows // TILE
    return pl.pallas_call(
        grads_kernel,
        out_shape=jax.ShapeDtypeStruct((n_rows, width), F32),
        grid_spec=pltpu.PrefetchScalarGridSpec(
            num_scalar_prefetch=2,
            grid=(n_tiles,),
            in_specs=[
                pl.BlockSpec((TILE, width), lambda t, ids, cnt: (t, 0)),
                pl.BlockSpec((TILE, width), lambda t, ids, cnt: (t, 0)),
                pl.BlockSpec((nb, rows, width), lambda t, ids, cnt: (0, 0, 0)),
                pl.BlockSpec((nb, 1, rows), lambda t, ids, cnt: (0, 0, 0)),
            ],
            out_specs=pl.BlockSpec((TILE, width), lambda t, ids, cnt: (t, 0)),
        ),
        input_output_aliases={2: 0},
        compiler_params=pltpu.CompilerParams(dimension_semantics=("arbitrary",)),
        cost_estimate=pl.CostEstimate(
            flops=nb * KMAX * 6 * 2 * rows * TILE * width // 2,
            transcendentals=nb * KMAX * rows * TILE // 2,
            bytes_accessed=3 * n_rows * width * 4 + nb * rows * width * 4,
        ),
    )(ids_flat, cnt, acc, items, seen_q, lse)


def positive_row(qblk, pblk, items, shard_at):
    local_rows = items.shape[0]
    offset = pblk - shard_at * local_rows
    inside = (offset >= 0) & (offset < local_rows)
    safe = jnp.clip(offset, 0, local_rows - 1)
    target = jnp.where(inside, offset, local_rows)
    chosen = jnp.take(items, safe, axis=0)
    logit = jnp.where(inside, jnp.sum(qblk * chosen, axis=1), 0.0)
    return (inside, target, chosen, logit)


def gather_packed(queries, positive, tile_ids, counts):
    rows, width = queries.shape
    n_shard = lax.axis_size("shard")
    pos_rows = rows // width
    ints = jnp.concatenate([tile_ids.reshape(-1), counts.reshape(-1)]).astype(jnp.float32)
    extra = jnp.zeros((8, width), jnp.float32)
    extra = extra.at[:pos_rows].set(positive.astype(jnp.float32).reshape(pos_rows, width))
    extra = extra.at[pos_rows, : ints.shape[0]].set(ints)
    packed = jnp.concatenate([queries, extra], axis=0)
    seen = lax.all_gather(packed, "shard")
    seen_q = seen[:, :rows]
    seen_pos = seen[:, rows : rows + pos_rows].reshape(n_shard, rows).astype(jnp.int32)
    n_ids = tile_ids.size
    flat = seen[:, rows + pos_rows].astype(jnp.int32)
    seen_ids = flat[:, :n_ids].reshape((n_shard,) + tile_ids.shape[1:])
    seen_cnt = flat[:, n_ids : n_ids + counts.size].reshape((n_shard,) + counts.shape[1:])
    return seen_q, seen_pos, seen_ids, seen_cnt


def local(queries, items, positive, tile_ids, counts):
    shard_at = lax.axis_index("shard")
    n_shard = lax.axis_size("shard")
    rows = queries.shape[0]
    width = queries.shape[1]
    seen_q, seen_pos, seen_ids, seen_cnt = gather_packed(queries, positive, tile_ids, counts)
    idrows = jnp.take(seen_ids, shard_at, axis=1)
    ids_flat = idrows.reshape(-1)
    cnt = jnp.take(seen_cnt, shard_at, axis=1)

    m_loc, l_loc, dq_u = block_stats(seen_q, items, ids_flat, cnt)
    m_loc = m_loc.reshape(n_shard, rows)
    l_loc = l_loc.reshape(n_shard, rows)

    inside, target, chosen, plog = positive_row(
        seen_q.reshape(-1, width), seen_pos.reshape(-1), items, shard_at
    )
    plog = plog.reshape(n_shard, rows)
    inside = inside.reshape(n_shard, rows)

    stacked = lax.all_gather(jnp.stack([m_loc, l_loc, plog]), "shard")
    tops, totals, plogs = stacked[:, 0], stacked[:, 1], stacked[:, 2]
    plogit = jnp.sum(plogs, axis=0)
    top = jnp.maximum(jnp.max(tops, axis=0), plogit)
    total = jnp.sum(totals * jnp.exp(tops - top[None]), axis=0) + jnp.exp(plogit - top)
    lse = top + jnp.log(total)
    loss = jnp.take(lse, shard_at, axis=0) - jnp.take(plogit, shard_at, axis=0)

    scale = jnp.exp(m_loc - lse)
    weight = jnp.where(inside, jnp.exp(plogit - lse) - 1.0, 0.0)
    dq_parts = scale[:, :, None] * dq_u + weight[:, :, None] * chosen.reshape(n_shard, rows, width)
    query_grad = lax.psum_scatter(dq_parts, "shard", scatter_dimension=0, tiled=True).reshape(
        rows, width
    )

    updates = weight.reshape(-1)[:, None] * seen_q.reshape(-1, width)
    d_local = jnp.zeros(items.shape, F32).at[target].add(updates, mode="drop")
    d_local = tile_grads(d_local, items, seen_q, lse.reshape(n_shard, 1, rows), ids_flat, cnt)
    item_grad = lax.psum_scatter(d_local, "dp", scatter_dimension=0, tiled=True)
    return (loss, query_grad, item_grad)


def solution(mesh):
    placed = (
        P(("dp", "shard"), None),
        P("shard", None),
        P(("dp", "shard")),
        P(("dp", "shard"), None, None),
        P(("dp", "shard"), None),
    )
    return jax.shard_map(
        local,
        mesh=mesh,
        in_specs=placed,
        out_specs=(P(("dp", "shard")), P(("dp", "shard"), None), P(("shard", "dp"), None)),
        check_vma=False,
    )
```

time: 815 us -> 518 us (0.64)
  matrix products: 140 us -> 0 us
  Pallas kernels: 0 us -> 110 us
  local copies, waits for them, and re-layouts: 117 us -> 27.4 us
  waiting for transfers between devices: 363 us -> 276 us
  loops' own time: 47 us -> 0 us
  other arithmetic: 96.2 us -> 58.3 us
    dot_general x56 -> x0, matrix products: 140 us -> none  [the longest x28 58.9 us: tile_logits(): jnp.einsum('qd,td->qt', qblk, block, precision=lax.Precision.HIGHEST, pre...]
    pallas_call x0 -> x2, Pallas kernels: none -> 110 us  [the longest x1 65.8 us: tile_grads(): pl.pallas_call(grads_kernel, out_shape=jax.ShapeDtypeStruct((n_rows, widt...]
    reduce_scatter x1, waiting for transfers between devices: 95.4 us -> 0.01 us  [local(): lax.psum_scatter(dq_parts, 'shard', scatter_dimension=0, tiled=True)]
    another operation x19 -> x0, loops' own time: 47 us -> none  [the longest x8 23.9 us: block_grads(): lax.fori_loop(0, count, visit, (jnp.zeros(qblk.shape, jnp.float32), d_loc...]
    gather x8 -> x1, local copies, waits for them, and re-layouts: 68.3 us -> 23.1 us  [positive_row(): chosen = jnp.take(items, safe, axis=0)]
    dynamic_update_slice x24 -> x0, other arithmetic: 39.5 us -> none  [local(): lax.map(stats_of, (seen_q, seen_pos, idrows, seen_counts))]
    dynamic_slice x60 -> x0, local copies, waits for them, and re-layouts: 26.3 us -> none  [the longest x16 9.25 us: local(): lax.map(stats_of, (seen_q, seen_pos, idrows, seen_counts))]
    reduce_sum x22 -> x2, other arithmetic: 13 us -> 0.04 us  [the longest x1 0.03 us: local(): jnp.sum(totals * jnp.exp(tops - top[None]), axis=0) + jnp.exp(plogit - top)]
  transfers between devices with their start and end apart: 3 -> 3, of which waited for: 3 -> 2; matrix products, arithmetic and copies ran while one was open for 5% -> 7% of each run, Pallas kernels for 0% -> 13%
where the time goes in v2:
time: 518 us; the launch traced here: 516 us
  waiting for transfers between devices  276 us (53%)
  Pallas kernels  110 us (21%)
  other arithmetic  58.3 us (11%)
  blocking collectives  30.4 us (6%)
  local copies, waits for them, and re-layouts  27.4 us (5%)
  between operations  13.9 us (3%)
    reduce_scatter x1, waiting for transfers between devices, local(): item_grad = lax.psum_scatter(d_local, 'dp', scatter_dimension=0, tiled=True)  182 us
    all_gather x1, waiting for transfers between devices, gather_packed(): seen = lax.all_gather(packed, 'shard')  94.3 us
    pallas_call x1, Pallas kernels, tile_grads(): pl.pallas_call(grads_kernel, out_shape=jax.ShapeDtypeStruct((n_rows, widt...  65.8 us
    pallas_call x1, Pallas kernels, block_stats(): pl.pallas_call(stats_kernel, out_shape=(jax.ShapeDtypeStruct((nb, rows, 1...  44.1 us
    scatter-add x1, other arithmetic, local(): d_local = jnp.zeros(items.shape, F32).at[target].add(updates, mode='drop')  31.2 us
    all_gather x1, blocking collectives, local(): stacked = lax.all_gather(jnp.stack([m_loc, l_loc, plog]), 'shard')  30.4 us
    gather x1, local copies, waits for them, and re-layouts, positive_row(): chosen = jnp.take(items, safe, axis=0)  23.1 us
  transfers between devices with their start and end apart: 3, of which 2 were waited for; matrix products, arithmetic and copies ran while one was open for 7% of the time, Pallas kernels for 13%

profile of v2, /device:TPU:1, one launch (start us, length us, event | category | flops | bytes accessed | tf_op | source)
XLA Modules:
  0.0 515.9 jit_solution(11932371973423196873)
XLA Ops:
  7.2 0.0 all-gather.4.cloned.1.call-start
  7.2 0.7 convert_element_type.54
  7.9 0.8 copy.29
  8.7 0.1 concatenate.17
  8.7 0.7 add_convert_fusion
  9.5 0.2 scatter.9
  9.7 1.9 pad_maximum_fusion
  11.6 0.0 reduce-scatter.3.cloned.1.call-start
  11.6 94.3 %all-gather.4.cloned.1.call-done = f32[4160,256]{1,0:T(8,128)} async-done(((f32[520,256]{1,0:T(8,128)}), f32[4160,256]{1,0:T(8,128)}) %all-gather.4.cloned.1.call-update) | async-done | bytes 4259856 | tf_op jit(solution)/shard_map/all_gather | solution.py:177
  105.9 0.9 slice_convert_fusion.1
  106.8 0.1 slice.94
  106.8 0.9 clamp_bitcast_fusion
  107.8 0.1 copy.30
  107.9 0.8 select_reduce_fusion.cnt_ref
  108.6 0.1 copy.31
  108.7 0.6 select_n.96.ids_ref
  109.3 0.1 compare_select_fusion
  109.4 23.1 %gather_fusion = f32[4096,256]{1,0:T(8,128)} fusion(f32[20480,256]{1,0:T(8,128)} %t_ref.3, s32[4096]{0:T(1024)S(1)} %broadcast_clamp_fusion), kind=kCustom, calls=%fused_computation | custom fusion | bytes 8404992 | tf_op jit(solution)/shard_map/jit(_take)/gather | solution.py:163
  132.5 5.5 %fusion.15 = (f32[8,512,256]{2,1,0:T(8,128)}, f32[8,512]{1,0:T(8,128)S(1)}) fusion(f32[8,520,256]{2,1,0:T(8,128)} %bitcast.78, f32[8,512,256]{2,1,0:T(8,128)} %bitcast.75, pred[8,512]{1,0:T(8,128)(4,1)S(1)} %compare_and_fusion.1), kind=kLoop, calls=%fused_computation.49 | loop fusion | flops 3141632 | bytes 12603392 | tf_op jit(solution)/shard_map/slice | solution.py:178
  138.0 44.1 %shard_map.76 = (f32[8,512,1]{2,1,0:T(8,128)}, f32[8,512,1]{2,1,0:T(8,128)}, f32[8,512,256]{2,1,0:T(8,128)}) custom-call(s32[24]{0:T(128)} %select_n.96.ids_ref, s32[8]{0:T(128)} %select_reduce_fusion.cnt_ref, f32[8,512,256]{2,1,0:T(8,128)} %get-tuple-element.71.q_ref, f32[20480,256]{1,0:T(8,128)} %t_ref.3), custom_call_target="tpu_custom_call" | custom-call | flops 19327352832 | bytes 20971520 | tf_op jit(solution)/shard_map/pallas_call | solution.py:70
  182.1 2.4 copy.33
  184.4 2.2 reduce.8
  186.7 0.6 reduce.9
  187.3 30.4 %all-gather.1 = f32[24,8,512]{2,1,0:T(8,128)S(1)} all-gather(f32[3,8,512]{2,1,0:T(8,128)S(1)} %pad_maximum_fusion.1), channel_id=3, replica_groups=mesh['dp'=16,'shard'=8] {'shard'}, dimensions={0}, use_global_device_ids=true | all-gather | bytes 442368 | tf_op jit(solution)/shard_map/all_gather | solution.py:207
  217.8 7.7 %multiply_add_fusion = f32[8,512,256]{2,1,0:T(8,128)} fusion(f32[8,512,256]{2,1,0:T(8,128)} %get-tuple-element.33, f32[8,512]{1,0:T(8,128)S(1)} %get-tuple-element.67, f32[8,512]{1,0:T(8,128)S(1)} %fusion.10, pred[8,512]{1,0:T(8,128)(4,1)S(1)} %compare_and_fusion.1, f32[4096,256]{1,0:T(8,128)} %gather_fusion), kind=kLoop, calls=%fused_computation.5 | loop fusion | flops 4194304 | bytes 12619776 | tf_op jit(solution)/shard_map/add | solution.py:217
  225.5 0.0 reduce-scatter.5.cloned.1.call-start
  225.7 3.9 bitcast_multiply_fusion
  229.6 31.2 %scatter_custom_fusion.acc_ref = f32[20480,256]{1,0:T(8,128)} fusion(s32[4096]{0:T(1024)S(1)} %bitcast.95, f32[4096,256]{1,0:T(8,128)} %bitcast_multiply_fusion, f32[]{:T(128)} %constant.119.clone.1), kind=kCustom, calls=%fused_computation.2 | custom fusion | flops 1048576 | bytes 20972032 | tf_op jit(solution)/shard_map/scatter-add | solution.py:223
  260.8 0.7 fusion.13.lse_ref
  261.4 65.8 %shard_map.77 = f32[20480,256]{1,0:T(8,128)} custom-call(s32[24]{0:T(128)} %select_n.96.ids_ref, s32[8]{0:T(128)} %select_reduce_fusion.cnt_ref, f32[20480,256]{1,0:T(8,128)} %scatter_custom_fusion.acc_ref, f32[20480,256]{1,0:T(8,128)} %t_ref.3, f32[8,512,256]{2,1,0:T(8,128)} %get-tuple-element.71.q_ref, ...), custom_call_target="tpu_custom_call", output_to_operand_aliasing={{}: (2, {})} | custom-call | flops 9663676416 | bytes 67108864 | tf_op jit(solution)/shard_map/pallas_call | solution.py:133
  327.3 0.6 sub.111
  327.9 181.5 %reduce-scatter.5.cloned.1.call-done = f32[1280,256]{1,0:T(8,128)} async-done(((f32[20480,256]{1,0:T(8,128)}), f32[1280,256]{1,0:T(8,128)}) %reduce-scatter.5.cloned.1.call-update) | async-done | bytes 1310736 | tf_op jit(solution)/shard_map/reduce_scatter | solution.py:225
  (34 shorter events, 0.4 us)
Async XLA Ops:
  7.2 98.7 %all-gather.4.cloned.1.call-start = ((), (), s32[]{:S(2)}) async-start(), calls=%async_computation.4 | async-start | bytes 4792320 | tf_op jit(solution)/shard_map/all_gather | solution.py:177
  11.6 316.3 %reduce-scatter.3.cloned.1.call-start = ((), (), s32[]{:S(2)}) async-start(), calls=%async_computation.2 | async-start | bytes 4718592 | tf_op jit(solution)/shard_map/reduce_scatter | solution.py:218
  182.1 4.6 copy-start
  225.5 283.8 %reduce-scatter.5.cloned.1.call-start = ((), (), s32[]{:S(2)}) async-start(), calls=%async_computation.3 | async-start | bytes 22282240 | tf_op jit(solution)/shard_map/reduce_scatter | solution.py:225
Sparse Core Ops, SparseCore 0:
  11.7 94.1 all-gather.3
  225.7 96.3 reduce-scatter.2
  327.4 181.9 reduce-scatter.4
